TPU v7x, 256 devices: a whole 4x4x8 slice. The times are simulated.
256 devices in a mesh: dp: 16 (over x, y_hi, core), expert: 16 (over z, y_lo).
Axes of the slice: x: 4, y: 4 (y_hi: 2, y_lo: 2; y = y_hi * 2 + y_lo), z: 8, core: 2. Of those that a mesh axis runs over, the one named last changes fastest.
Arguments:
- tokens: bfloat16 [2048, 4096], P('expert', 'dp'), may hold values from -6 to 6
- expert_ids: int32 [2048, 8], P('expert'), may hold values from 0 to 63, all different within a row; in each aligned block of 128 rows (0 to 127, 128 to 255, ...) at most 32 rows name the same one
- gate_prob: float32 [2048, 8], P('expert'), may hold values from 0.05 to 0.35
- w_gate: bfloat16 [64, 4096, 768], P('expert', 'dp'), may hold values from -0.09375 to 0.09375
- w_up: bfloat16 [64, 4096, 768], P('expert', 'dp'), may hold values from -0.09375 to 0.09375
- w_down: bfloat16 [64, 768, 4096], P('expert', None, 'dp'), may hold values from -0.21875 to 0.21875
- grad_out: bfloat16 [2048, 4096], P('expert', 'dp'), may hold values from -6 to 6
Outputs:
- mixed: bfloat16 [2048, 4096], P('expert', 'dp')
- grad_tokens: bfloat16 [2048, 4096], P('expert', 'dp')
- grad_gate: float32 [2048, 8], P('expert')
- grad_w_gate: bfloat16 [64, 4096, 768], P('expert', 'dp')
- grad_w_up: bfloat16 [64, 4096, 768], P('expert', 'dp')
- grad_w_down: bfloat16 [64, 768, 4096], P('expert', None, 'dp')
Inputs may be any that keep to these rules, and one draw needn't show every extreme that they name: `expert_ids`: each row names 8 different experts. Within the rows of one index of expert (aligned blocks of 128 rows) no expert is named by more than 32 rows, a bound that some block reaches.
All inputs are finite; a program needn't handle non-finite values.
Results may differ from a plain program's by a relative error of at most 0.035.
Values may be sent and summed in bfloat16 or wider, within the bound.
No kernel may reach another device: no remote copies, remote signals or barrier semaphores. Data moves between devices by JAX's collectives and lax.ppermute only.
A program may use at most 128 MiB of HBM per device.

v0:
```python
import jax
import jax.numpy as jnp
from jax import lax
from jax.sharding import PartitionSpec as P


def slot_tables(expert_ids, columns, per_device, capacity):
    flat_ids = expert_ids.reshape(-1)
    assign_count = flat_ids.shape[0]
    experts_all = columns * per_device
    onehot = (flat_ids[:, None] == jnp.arange(experts_all, dtype=jnp.int32)[None, :]).astype(
        jnp.int32
    )
    before = jnp.cumsum(onehot, axis=0) - onehot
    rank_in = jnp.sum(before * onehot, axis=1)
    slot_of = (flat_ids % per_device * columns + flat_ids // per_device) * capacity + rank_in
    slot_count = experts_all * capacity
    source = (
        jnp.full((slot_count,), assign_count, jnp.int32)
        .at[slot_of]
        .set(jnp.arange(assign_count, dtype=jnp.int32))
    )
    return (slot_of, source)


def run_groups(bundles, hidden_units):
    parties = lax.axis_size("dp")
    row_totals = [bundle[0].shape[0] * bundle[0].shape[1] for bundle in bundles]
    gate_part = jnp.concatenate(
        [
            jnp.einsum(
                "grd,gdf->grf", bundle[0], bundle[2], preferred_element_type=jnp.float32
            ).reshape(-1, hidden_units)
            for bundle in bundles
        ],
        axis=0,
    )
    up_part = jnp.concatenate(
        [
            jnp.einsum(
                "grd,gdf->grf", bundle[0], bundle[3], preferred_element_type=jnp.float32
            ).reshape(-1, hidden_units)
            for bundle in bundles
        ],
        axis=0,
    )
    total_rows = gate_part.shape[0]
    share_rows = total_rows // parties
    share_start = lax.axis_index("dp") * share_rows
    gate_pre, up_pre = (
        lax.psum(gate_part.astype(jnp.bfloat16), "dp").astype(jnp.float32),
        lax.psum(up_part.astype(jnp.bfloat16), "dp").astype(jnp.float32),
    )
    hidden = (jax.nn.silu(gate_pre) * up_pre).astype(jnp.bfloat16)
    gate_share = lax.dynamic_slice_in_dim(gate_pre, share_start, share_rows, 0)
    up_share = lax.dynamic_slice_in_dim(up_pre, share_start, share_rows, 0)
    hidden_part = jnp.concatenate(
        [
            jnp.einsum(
                "grd,gfd->grf", bundle[1], bundle[4], preferred_element_type=jnp.float32
            ).reshape(-1, hidden_units)
            for bundle in bundles
        ],
        axis=0,
    )
    hidden_grad = lax.psum_scatter(
        hidden_part.astype(jnp.bfloat16), "dp", scatter_dimension=0, tiled=True
    ).astype(jnp.float32)
    sigmoid_g = jax.nn.sigmoid(gate_share)
    gate_grad = (
        hidden_grad * up_share * sigmoid_g * (1.0 + gate_share * (1.0 - sigmoid_g))
    ).astype(jnp.bfloat16)
    up_grad = (hidden_grad * gate_share * sigmoid_g).astype(jnp.bfloat16)
    gate_rows, up_rows = (
        lax.all_gather(gate_grad, "dp", axis=0, tiled=True),
        lax.all_gather(up_grad, "dp", axis=0, tiled=True),
    )
    outputs = []
    offset = 0
    for bundle, row_total in zip(bundles, row_totals):
        piece_shape = (bundle[0].shape[0], bundle[0].shape[1], hidden_units)
        hidden_piece = hidden.reshape(piece_shape)
        gate_piece = gate_rows.reshape(piece_shape)
        up_piece = up_rows.reshape(piece_shape)
        offset = offset + row_total
        expert_out = jnp.einsum(
            "grf,gfd->grd", hidden_piece, bundle[4], preferred_element_type=jnp.float32
        ).astype(jnp.bfloat16)
        slot_grad = (
            jnp.einsum("grf,gdf->grd", gate_piece, bundle[2], preferred_element_type=jnp.float32)
            + jnp.einsum("grf,gdf->grd", up_piece, bundle[3], preferred_element_type=jnp.float32)
        ).astype(jnp.bfloat16)
        dw_gate = jnp.einsum(
            "grd,grf->gdf", bundle[0], gate_piece, preferred_element_type=jnp.float32
        )
        dw_up = jnp.einsum("grd,grf->gdf", bundle[0], up_piece, preferred_element_type=jnp.float32)
        dw_down = jnp.einsum(
            "grf,grd->gfd", hidden_piece, bundle[1], preferred_element_type=jnp.float32
        )
        outputs.append((expert_out, slot_grad, dw_gate, dw_up, dw_down))
    return outputs


def on_device(tokens, expert_ids, gate_prob, w_gate, w_up, w_down, grad_out):
    tok_rows, fanout = expert_ids.shape
    per_device, slice_width, hidden_units = w_gate.shape
    columns = lax.axis_size("expert")
    capacity = 2 * tok_rows * fanout // (per_device * columns)
    slot_count = per_device * columns * capacity
    assign_count = tok_rows * fanout
    slot_of, source = slot_tables(expert_ids, columns, per_device, capacity)
    filled = source < assign_count
    safe_src = jnp.minimum(source, assign_count - 1)
    tok_index = safe_src // fanout
    gate_flat = gate_prob.reshape(-1)
    token_buffer = jnp.where(filled[:, None], tokens[tok_index], jnp.zeros((), jnp.bfloat16))
    gate_slots = jnp.where(filled, gate_flat[safe_src], jnp.zeros((), jnp.float32))
    grad_buffer = (gate_slots[:, None] * grad_out[tok_index].astype(jnp.float32)).astype(
        jnp.bfloat16
    )
    layout = (per_device, columns, capacity, slice_width)
    sent_tokens, sent_grads = (
        lax.all_to_all(
            token_buffer.reshape(layout), "expert", split_axis=1, concat_axis=1, tiled=True
        ),
        lax.all_to_all(
            grad_buffer.reshape(layout), "expert", split_axis=1, concat_axis=1, tiled=True
        ),
    )
    bundles = [
        (
            sent_tokens.reshape(per_device, columns * capacity, slice_width),
            sent_grads.reshape(per_device, columns * capacity, slice_width),
            w_gate,
            w_up,
            w_down,
        )
    ]
    results = run_groups(bundles, hidden_units)
    expert_out = results[0][0].reshape(layout)
    slot_grad = results[0][1].reshape(layout)
    total_gate = results[0][2]
    total_up = results[0][3]
    total_down = results[0][4]
    grad_w_gate = total_gate.astype(jnp.bfloat16)
    grad_w_up = total_up.astype(jnp.bfloat16)
    grad_w_down = total_down.astype(jnp.bfloat16)
    back_out, back_grad = (
        lax.all_to_all(expert_out, "expert", split_axis=1, concat_axis=1, tiled=True),
        lax.all_to_all(slot_grad, "expert", split_axis=1, concat_axis=1, tiled=True),
    )
    out_rows = (
        back_out.reshape(slot_count, slice_width)[slot_of]
        .reshape(tok_rows, fanout, slice_width)
        .astype(jnp.float32)
    )
    grad_rows = (
        back_grad.reshape(slot_count, slice_width)[slot_of]
        .reshape(tok_rows, fanout, slice_width)
        .astype(jnp.float32)
    )
    mixed = jnp.sum(gate_prob[:, :, None] * out_rows, axis=1).astype(jnp.bfloat16)
    grad_tokens = jnp.sum(grad_rows, axis=1).astype(jnp.bfloat16)
    partial_dots = jnp.sum(out_rows * grad_out.astype(jnp.float32)[:, None, :], axis=2)
    grad_gate = lax.psum(partial_dots, "dp")
    return (mixed, grad_tokens, grad_gate, grad_w_gate, grad_w_up, grad_w_down)


def solution(mesh):
    return jax.shard_map(
        on_device,
        mesh=mesh,
        in_specs=(
            P("expert", "dp"),
            P("expert", None),
            P("expert", None),
            P("expert", "dp", None),
            P("expert", "dp", None),
            P("expert", None, "dp"),
            P("expert", "dp"),
        ),
        out_specs=(
            P("expert", "dp"),
            P("expert", "dp"),
            P("expert", None),
            P("expert", "dp", None),
            P("expert", "dp", None),
            P("expert", None, "dp"),
        ),
        check_vma=False,
    )
```

profile of v0, /device:TPU:32, one launch (start us, length us, event | category | flops | bytes accessed | tf_op | source)
XLA Modules:
  0.0 592.9 jit_solution(16468973395299543634)
XLA Ops:
  7.2 0.0 copy-start
  7.2 0.0 all-reduce.3.cloned.1.call-start
  7.2 0.9 copy.47
  8.1 0.1 eq.31
  8.2 0.1 eq.27
  8.3 0.1 reshape.224
  8.4 0.8 copy.46
  9.2 0.1 reshape.230
  9.3 18.0 %reduce-window.6 = s32[64,8,128]{2,1,0:T(8,128)S(1)} reduce-window(s32[64,8,128]{2,1,0:T(8,128)S(1)} %fusion.11, s32[]{:T(128)} %constant.58.clone.1), window={size=1x1x128 pad=0_0x0_0x127_0}, to_apply=%region_0.0 | reduce-window | flops 8323072 | bytes 524292 | tf_op jit(solution)/shard_map/reduce-window
  27.3 0.1 slice.18
  27.5 0.1 copy.50
  27.6 0.1 copy.51
  27.7 0.1 broadcast_add_fusion
  27.9 0.1 fusion.10
  28.0 4.3 scatter_custom_fusion
  32.4 8.6 %gather_fusion.2 = f32[2048]{0:T(1024)S(1)} fusion(f32[1024]{0:T(1024)S(1)} %reshape.230, s32[2048]{0:T(1024)S(1)} %get-tuple-element.26), kind=kCustom, calls=%fused_computation.2 | custom fusion | bytes 24576 | tf_op jit(solution)/shard_map/gather | solution.py:117
  41.0 0.1 broadcast_in_dim.33
  41.1 7.5 %gather_fusion = bf16[2048,256]{1,0:T(8,128)(2,1)S(1)} fusion(bf16[128,256]{1,0:T(8,128)(2,1)S(1)} %copy-done.2, s32[2048]{0:T(1024)S(1)} %get-tuple-element.27), kind=kCustom, calls=%fused_computation | custom fusion | bytes 2105344 | tf_op jit(solution)/shard_map/gather | solution.py:116
  48.6 0.4 copy_select_fusion
  49.1 35.7 %all_to_all.20 = bf16[4,16,32,256]{3,2,0,1:T(8,128)(2,1)S(1)} all-to-all(bf16[4,16,32,256]{3,2,0,1:T(8,128)(2,1)S(1)} %copy_select_fusion), channel_id=1, replica_groups=mesh['dp'=16,'expert'=16] {'expert'}, dimensions={1} | all-to-all | bytes 2097152 | tf_op jit(solution)/shard_map/all_to_all | solution.py:123
  84.7 0.1 copy.54
  84.9 2.6 convolution_convert_fusion.1
  87.5 2.6 convolution_convert_fusion.2
  90.2 0.0 all-reduce.3.cloned.1.call-update
  90.2 0.0 reduce-scatter.2.cloned.1.call-start
  90.2 0.1 mul.97
  90.3 0.7 copy-done.1
  91.0 7.5 %gather_fusion.3 = bf16[2048,256]{1,0:T(8,128)(2,1)S(1)} fusion(bf16[128,256]{1,0:T(8,128)(2,1)S(1)} %copy-done.1, s32[2048]{0:T(1024)S(1)} %get-tuple-element.27), kind=kCustom, calls=%fused_computation.3 | custom fusion | bytes 2105344 | tf_op jit(solution)/shard_map/gather | solution.py:118
  98.5 0.3 fusion
  98.8 32.5 %all_to_all.21 = bf16[4,16,32,256]{3,2,0,1:T(8,128)(2,1)S(1)} all-to-all(bf16[4,16,32,256]{3,2,0,1:T(8,128)(2,1)S(1)} %fusion), channel_id=1, replica_groups=mesh['dp'=16,'expert'=16] {'expert'}, dimensions={1} | all-to-all | bytes 2097152 | tf_op jit(solution)/shard_map/all_to_all | solution.py:126
  131.3 0.1 copy.60
  131.4 2.7 convolution_convert_fusion
  134.1 0.0 reduce-scatter.2.cloned.1.call-update
  134.2 0.0 all-gather.3.cloned.1.call-start
  134.2 139.9 %all-reduce.3.cloned.1.call-done = (bf16[2048,768]{1,0:T(8,128)(2,1)}, bf16[2048,768]{1,0:T(8,128)(2,1)}) async-done(((bf16[2048,768]{1,0:T(8,128)(2,1)}, bf16[2048,768]{1,0:T(8,128)(2,1)}), (bf16[2048,768]{1,0:T(8,128)(2,1)}, bf16[2048,768]{1,0:T(8,128)(2,1)})) %all-reduce.3.cloned.1.call-update) | async-done | bytes 6291472 | tf_op jit(solution)/shard_map/psum | solution.py:52
  274.1 5.2 convert_element_type.91
  279.3 3.1 convert_element_type.94
  282.4 79.0 %reduce-scatter.2.cloned.1.call-done = bf16[128,768]{1,0:T(8,128)(2,1)} async-done(((bf16[2048,768]{1,0:T(8,128)(2,1)}), bf16[128,768]{1,0:T(8,128)(2,1)}) %reduce-scatter.2.cloned.1.call-update) | async-done | bytes 196624 | tf_op jit(solution)/shard_map/reduce_scatter | solution.py:66
  361.5 2.1 fusion.7
  363.6 0.0 all-gather.3.cloned.1.call-update
  363.6 0.0 all-gather.5.cloned.1.call-start
  363.7 0.5 all-gather.5.cloned.1.call-update
  364.2 3.8 multiply_convert_fusion
  368.1 1.0 convolution_convert_fusion.6
  369.1 0.7 copy-done.7
  369.8 1.0 copy.55
  370.8 7.5 %all-to-all-start.1 = ((bf16[4,16,32,256]{3,2,0,1:T(8,128)(2,1)}), bf16[4,16,32,256]{3,2,0,1:T(8,128)(2,1)}, u32[]{:S(2)}, u32[]{:S(2)}) async-start(bf16[4,16,32,256]{3,2,0,1:T(8,128)(2,1)} %copy.55), calls=%async_computation.1 | async-start | bytes 2097152 | tf_op jit(solution)/shard_map/all_to_all | solution.py:149
  378.3 42.8 %all-gather.3.cloned.1.call-done = bf16[2048,768]{1,0:T(8,128)(2,1)} async-done(((bf16[128,768]{1,0:T(8,128)(2,1)}), bf16[2048,768]{1,0:T(8,128)(2,1)}) %all-gather.3.cloned.1.call-update) | async-done | bytes 3145744 | tf_op jit(solution)/shard_map/all_gather | solution.py:75
  421.1 4.7 fusion.20
  425.8 54.7 %all-gather.5.cloned.1.call-done = bf16[2048,768]{1,0:T(8,128)(2,1)} async-done(((bf16[128,768]{1,0:T(8,128)(2,1)}), bf16[2048,768]{1,0:T(8,128)(2,1)}) %all-gather.5.cloned.1.call-update) | async-done | bytes 3145744 | tf_op jit(solution)/shard_map/all_gather | solution.py:76
  480.5 4.0 add_convert_fusion
  484.5 1.1 copy.61
  485.6 7.5 %all-to-all-start.3 = ((bf16[4,16,32,256]{3,2,0,1:T(8,128)(2,1)}), bf16[4,16,32,256]{3,2,0,1:T(8,128)(2,1)}, u32[]{:S(2)}, u32[]{:S(2)}) async-start(bf16[4,16,32,256]{3,2,0,1:T(8,128)(2,1)} %copy.61), calls=%async_computation.4 | async-start | bytes 2097152 | tf_op jit(solution)/shard_map/all_to_all | solution.py:150
  493.1 4.3 convolution_convert_fusion.3
  497.4 1.3 copy.56
  498.7 3.9 gather_fusion.1
  502.7 1.1 fusion.2
  503.8 69.0 %psum.23 = f32[128,8]{1,0:T(8,128)S(1)} all-reduce(f32[128,8]{1,0:T(8,128)S(1)} %get-tuple-element.18), channel_id=1, replica_groups=mesh['dp'=16,'expert'=16] {'dp'}, use_global_device_ids=true, to_apply=%region_10.11 | all-reduce | flops 1024 | bytes 8192 | tf_op jit(solution)/shard_map/psum | solution.py:165
  572.8 0.7 copy.66
  573.4 4.5 convolution_convert_fusion.5
  578.0 2.2 convolution_convert_fusion.4
  580.2 1.3 copy.62
  581.5 3.9 gather_fusion.4
  585.4 1.0 bitcast_reduce_fusion
  (30 shorter events, 0.2 us)
Async XLA Ops:
  7.2 124.3 %copy-start = (bf16[4,768,256]{2,1,0:T(8,128)(2,1)S(1)}, bf16[4,768,256]{2,1,0:T(8,128)(2,1)}, u32[]{:S(2)}) copy-start(bf16[4,768,256]{2,1,0:T(8,128)(2,1)} %param.12) | copy-start | bytes 4718596
  7.2 266.9 %all-reduce.3.cloned.1.call-start = ((), (), s32[]{:S(2)}) async-start(), calls=%async_computation.8 | async-start | bytes 12582912 | tf_op jit(solution)/shard_map/psum | solution.py:52
  32.4 8.7 %copy-start.2 = (bf16[128,256]{1,0:T(8,128)(2,1)S(1)}, bf16[128,256]{1,0:T(8,128)(2,1)}, u32[]{:S(2)}) copy-start(bf16[128,256]{1,0:T(8,128)(2,1)} %param.7) | copy-start | bytes 196612
  48.6 36.3 %copy-start.9 = (bf16[4,256,768]{2,1,0:T(8,128)(2,1)S(1)}, bf16[4,256,768]{2,1,0:T(8,128)(2,1)}, u32[]{:S(2)}) copy-start(bf16[4,256,768]{2,1,0:T(8,128)(2,1)} %param.11) | copy-start | bytes 4718596
  84.8 5.3 copy-start.3
  84.8 2.7 copy-start.8
  90.2 0.8 copy-start.1
  90.2 271.3 %reduce-scatter.2.cloned.1.call-start = ((), (), s32[]{:S(2)}) async-start(), calls=%async_computation.5 | async-start | bytes 3342336 | tf_op jit(solution)/shard_map/reduce_scatter | solution.py:66
  134.2 287.0 %all-gather.3.cloned.1.call-start = ((), (), s32[]{:S(2)}) async-start(), calls=%async_computation.6 | async-start | bytes 3342336 | tf_op jit(solution)/shard_map/all_gather | solution.py:75
  274.1 5.2 copy-start.5
  363.6 116.8 %all-gather.5.cloned.1.call-start = ((), (), s32[]{:S(2)}) async-start(), calls=%async_computation.7 | async-start | bytes 3342336 | tf_op jit(solution)/shard_map/all_gather | solution.py:76
  368.1 1.7 copy-start.7
  370.8 114.8 %all-to-all-start.1 = ((bf16[4,16,32,256]{3,2,0,1:T(8,128)(2,1)}), bf16[4,16,32,256]{3,2,0,1:T(8,128)(2,1)}, u32[]{:S(2)}, u32[]{:S(2)}) async-start(bf16[4,16,32,256]{3,2,0,1:T(8,128)(2,1)} %copy.55), calls=%async_computation.1 | async-start | bytes 2097152 | tf_op jit(solution)/shard_map/all_to_all | solution.py:149
  485.6 94.6 %all-to-all-start.3 = ((bf16[4,16,32,256]{3,2,0,1:T(8,128)(2,1)}), bf16[4,16,32,256]{3,2,0,1:T(8,128)(2,1)}, u32[]{:S(2)}, u32[]{:S(2)}) async-start(bf16[4,16,32,256]{3,2,0,1:T(8,128)(2,1)} %copy.61), calls=%async_computation.4 | async-start | bytes 2097152 | tf_op jit(solution)/shard_map/all_to_all | solution.py:150
  503.8 74.2 %copy-start.4 = (bf16[4,16,32,256]{3,2,1,0:T(8,128)(2,1)S(1)}, bf16[4,16,32,256]{3,2,1,0:T(8,128)(2,1)}, u32[]{:S(2)}) copy-start(bf16[4,16,32,256]{3,2,1,0:T(8,128)(2,1)} %copy-done.3) | copy-start | bytes 3145732
  573.4 4.5 copy-start.6
Sparse Core Ops, SparseCore 0:
  90.3 183.7 all-reduce.2
  278.4 83.0 reduce-scatter.1
  364.2 56.9 all-gather.2
  424.2 56.2 all-gather.4
where the time goes:
time: 594 us; the launch traced here: 593 us
  waiting for transfers between devices  317 us (53%)
  blocking collectives  137 us (23%)
  local copies, waits for them, and re-layouts  45.3 us (8%)
  other arithmetic  35.5 us (6%)
  matrix products  28.7 us (5%)
  starting transfers between devices  15.2 us (3%)
  between operations  14.1 us (2%)
    psum x1, waiting for transfers between devices, run_groups(): lax.psum(up_part.astype(jnp.bfloat16), 'dp').astype(jnp.float32)  140 us
    reduce_scatter x1, waiting for transfers between devices, run_groups(): lax.psum_scatter(hidden_part.astype(jnp.bfloat16), 'dp', scatter_dimensio...  79 us
    psum x1, blocking collectives, on_device(): grad_gate = lax.psum(partial_dots, 'dp')  69 us
    all_gather x1, waiting for transfers between devices, run_groups(): lax.all_gather(up_grad, 'dp', axis=0, tiled=True)  54.7 us
    all_gather x1, waiting for transfers between devices, run_groups(): lax.all_gather(gate_grad, 'dp', axis=0, tiled=True)  42.8 us
    all_to_all x1, blocking collectives, on_device(): lax.all_to_all(token_buffer.reshape(layout), 'expert', split_axis=1, conc...  35.7 us
    all_to_all x1, blocking collectives, on_device(): lax.all_to_all(grad_buffer.reshape(layout), 'expert', split_axis=1, conca...  32.5 us
    another operation x3, other arithmetic  18.2 us
  transfers between devices with their start and end apart: 6, of which 4 were waited for; matrix products, arithmetic and copies ran while one was open for 9% of the time, Pallas kernels for 0%

commit v1 on v0

--- a/solution.py
+++ b/solution.py
@@ -49,7 +49,7 @@
     share_start = lax.axis_index("dp") * share_rows
     gate_pre, up_pre = (
         lax.psum(gate_part.astype(jnp.bfloat16), "dp").astype(jnp.float32),
-        lax.psum(up_part.astype(jnp.bfloat16), "dp").astype(jnp.float32),
+        jnp.sum(lax.all_gather(up_part.astype(jnp.bfloat16), "dp"), axis=0).astype(jnp.float32),
     )
     hidden = (jax.nn.silu(gate_pre) * up_pre).astype(jnp.bfloat16)
     gate_share = lax.dynamic_slice_in_dim(gate_pre, share_start, share_rows, 0)

time: 594 us -> 836 us (1.41)
  waiting for transfers between devices: 317 us -> 539 us
  other arithmetic: 35.5 us -> 56.5 us
    all_gather x0 -> x1, waiting for transfers between devices: none -> 269 us  [run_groups(): lax.all_gather(up_part.astype(jnp.bfloat16), 'dp')]
    psum x1, waiting for transfers between devices: 140 us -> 112 us  [run_groups(): lax.psum(gate_part.astype(jnp.bfloat16), 'dp').astype(jnp.float32)]
    reduce_sum x0 -> x1, other arithmetic: none -> 19.1 us  [run_groups(): jnp.sum(lax.all_gather(up_part.astype(jnp.bfloat16), 'dp'), axis=0)]
    reduce_scatter x1, waiting for transfers between devices: 79 us -> 60.4 us  [run_groups(): lax.psum_scatter(hidden_part.astype(jnp.bfloat16), 'dp', scatter_dimensio...]
  transfers between devices with their start and end apart: 6 -> 7, of which waited for: 4 -> 5; matrix products, arithmetic and copies ran while one was open for 9% -> 9% of each run, Pallas kernels for 0% -> 0%
where the time goes in v1:
time: 836 us
  waiting for transfers between devices  539 us (64%)
  blocking collectives  136 us (16%)
  other arithmetic  56.5 us (7%)
  local copies, waits for them, and re-layouts  44.7 us (5%)
  matrix products  30 us (4%)
  starting transfers between devices  15.2 us (2%)
  between operations  14.1 us (2%)
    all_gather x1, waiting for transfers between devices, run_groups(): lax.all_gather(up_part.astype(jnp.bfloat16), 'dp')  269 us
    psum x1, waiting for transfers between devices, run_groups(): lax.psum(gate_part.astype(jnp.bfloat16), 'dp').astype(jnp.float32)  112 us
    psum x1, blocking collectives, on_device(): grad_gate = lax.psum(partial_dots, 'dp')  69 us
    reduce_scatter x1, waiting for transfers between devices, run_groups(): lax.psum_scatter(hidden_part.astype(jnp.bfloat16), 'dp', scatter_dimensio...  60.4 us
    all_gather x1, waiting for transfers between devices, run_groups(): lax.all_gather(up_grad, 'dp', axis=0, tiled=True)  54.7 us
    all_gather x1, waiting for transfers between devices, run_groups(): lax.all_gather(gate_grad, 'dp', axis=0, tiled=True)  42.5 us
    all_to_all x1, blocking collectives, on_device(): lax.all_to_all(token_buffer.reshape(layout), 'expert', split_axis=1, conc...  35.7 us
    all_to_all x1, blocking collectives, on_device(): lax.all_to_all(grad_buffer.reshape(layout), 'expert', split_axis=1, conca...  31.4 us
  transfers between devices with their start and end apart: 7, of which 5 were waited for; matrix products, arithmetic and copies ran while one was open for 9% of the time, Pallas kernels for 0%

profile of v1, /device:TPU:32, one launch (start us, length us, event | category | flops | bytes accessed | tf_op | source)
XLA Modules:
  0.0 835.6 jit_solution(2381519533392355521)
XLA Ops:
  7.2 0.0 all-reduce.2.cloned.1.call-start
  7.2 0.9 copy.47
  8.1 0.1 eq.31
  8.2 0.1 eq.27
  8.3 0.1 reshape.234
  8.4 18.0 %reduce-window.6 = s32[64,8,128]{2,1,0:T(8,128)S(1)} reduce-window(s32[64,8,128]{2,1,0:T(8,128)S(1)} %fusion.11, s32[]{:T(128)} %constant.59.clone.1), window={size=1x1x128 pad=0_0x0_0x127_0}, to_apply=%region_0.0 | reduce-window | flops 8323072 | bytes 524292 | tf_op jit(solution)/shard_map/reduce-window
  26.4 0.1 slice.18
  26.6 0.1 copy.50
  26.8 0.1 copy.51
  26.9 0.1 broadcast_add_fusion
  27.0 0.1 fusion.10
  27.1 4.3 scatter_custom_fusion
  31.5 0.8 copy.46
  32.3 0.1 reshape.240
  32.4 8.6 %gather_fusion.2 = f32[2048]{0:T(1024)S(1)} fusion(f32[1024]{0:T(1024)S(1)} %reshape.240, s32[2048]{0:T(1024)S(1)} %get-tuple-element.24), kind=kCustom, calls=%fused_computation.2 | custom fusion | bytes 24576 | tf_op jit(solution)/shard_map/gather | solution.py:117
  41.0 0.1 broadcast_in_dim.33
  41.1 7.5 gather_fusion
  48.6 0.4 copy_select_fusion
  49.1 35.7 %all_to_all.20 = bf16[4,16,32,256]{3,2,0,1:T(8,128)(2,1)S(1)} all-to-all(bf16[4,16,32,256]{3,2,0,1:T(8,128)(2,1)S(1)} %copy_select_fusion), channel_id=1, replica_groups=mesh['dp'=16,'expert'=16] {'expert'}, dimensions={1} | all-to-all | bytes 2097152 | tf_op jit(solution)/shard_map/all_to_all | solution.py:123
  84.7 0.1 copy.54
  84.9 2.6 convolution_convert_fusion.2
  87.5 0.0 all-reduce.2.cloned.1.call-update
  87.5 0.0 all-gather.4.cloned.1.call-start
  87.6 4.0 convolution_convert_fusion.1
  91.6 0.0 all-gather.4.cloned.1.call-update
  91.6 0.0 reduce-scatter.2.cloned.1.call-start
  91.6 0.1 mul.97
  91.7 7.5 gather_fusion.3
  99.2 0.3 fusion
  99.6 31.4 %all_to_all.21 = bf16[4,16,32,256]{3,2,0,1:T(8,128)(2,1)S(1)} all-to-all(bf16[4,16,32,256]{3,2,0,1:T(8,128)(2,1)S(1)} %fusion), channel_id=1, replica_groups=mesh['dp'=16,'expert'=16] {'expert'}, dimensions={1} | all-to-all | bytes 2097152 | tf_op jit(solution)/shard_map/all_to_all | solution.py:126
  131.0 0.1 copy.60
  131.1 2.7 convolution_convert_fusion
  133.8 0.0 all-gather.6.cloned.1.call-start
  133.9 112.0 %all-reduce.2.cloned.1.call-done = bf16[2048,768]{1,0:T(8,128)(2,1)} async-done(((bf16[2048,768]{1,0:T(8,128)(2,1)}), bf16[2048,768]{1,0:T(8,128)(2,1)}) %all-reduce.2.cloned.1.call-update) | async-done | bytes 3145744 | tf_op jit(solution)/shard_map/psum | solution.py:51
  245.8 5.0 convert_element_type.100
  250.8 268.9 %all-gather.4.cloned.1.call-done = bf16[16,2048,768]{2,1,0:T(8,128)(2,1)} async-done(((bf16[1,2048,768]{2,1,0:T(8,128)(2,1)}), bf16[16,2048,768]{2,1,0:T(8,128)(2,1)}) %all-gather.4.cloned.1.call-update) | async-done | bytes 50331664 | tf_op jit(solution)/shard_map/all_gather | solution.py:52
  519.7 19.1 %reduce_sum.55 = bf16[2048,768]{1,0:T(8,128)(2,1)} reduce(bf16[16,2048,768]{2,1,0:T(8,128)(2,1)} %all-gather.4.cloned.1.call-done, bf16[]{:T(256)} %constant.71.clone.1), dimensions={0}, to_apply=%region_5.6 | reduce | flops 23592960 | bytes 53477376 | tf_op jit(solution)/shard_map/reduce_sum | solution.py:52
  538.8 5.2 convert_element_type.103
  544.0 60.4 %reduce-scatter.2.cloned.1.call-done = bf16[128,768]{1,0:T(8,128)(2,1)} async-done(((bf16[2048,768]{1,0:T(8,128)(2,1)}), bf16[128,768]{1,0:T(8,128)(2,1)}) %reduce-scatter.2.cloned.1.call-update) | async-done | bytes 196624 | tf_op jit(solution)/shard_map/reduce_scatter | solution.py:66
  604.4 2.1 fusion.7
  606.6 0.0 all-gather.8.cloned.1.call-start
  606.6 0.5 all-gather.8.cloned.1.call-update
  607.2 3.8 multiply_convert_fusion
  611.0 1.0 convolution_convert_fusion.6
  612.0 0.7 copy-done.6
  612.7 1.0 copy.55
  613.7 7.5 all-to-all-start.1
  621.3 42.5 %all-gather.6.cloned.1.call-done = bf16[2048,768]{1,0:T(8,128)(2,1)} async-done(((bf16[128,768]{1,0:T(8,128)(2,1)}), bf16[2048,768]{1,0:T(8,128)(2,1)}) %all-gather.6.cloned.1.call-update) | async-done | bytes 3145744 | tf_op jit(solution)/shard_map/all_gather | solution.py:75
  663.8 4.7 fusion.20
  668.5 54.7 %all-gather.8.cloned.1.call-done = bf16[2048,768]{1,0:T(8,128)(2,1)} async-done(((bf16[128,768]{1,0:T(8,128)(2,1)}), bf16[2048,768]{1,0:T(8,128)(2,1)}) %all-gather.8.cloned.1.call-update) | async-done | bytes 3145744 | tf_op jit(solution)/shard_map/all_gather | solution.py:76
  723.2 4.0 add_convert_fusion
  727.2 1.1 copy.61
  728.3 7.5 all-to-all-start.3
  735.8 4.3 convolution_convert_fusion.3
  740.1 1.3 copy.56
  741.4 3.9 gather_fusion.1
  745.3 1.1 fusion.2
  746.5 69.0 %psum.15 = f32[128,8]{1,0:T(8,128)S(1)} all-reduce(f32[128,8]{1,0:T(8,128)S(1)} %get-tuple-element.18), channel_id=1, replica_groups=mesh['dp'=16,'expert'=16] {'dp'}, use_global_device_ids=true, to_apply=%region_10.11 | all-reduce | flops 1024 | bytes 8192 | tf_op jit(solution)/shard_map/psum | solution.py:165
  815.4 0.7 copy.66
  816.1 4.5 convolution_convert_fusion.4
  820.6 2.2 convolution_convert_fusion.5
  822.8 1.3 copy.62
  824.1 3.9 gather_fusion.4
  828.1 1.0 bitcast_reduce_fusion
  (30 shorter events, 0.2 us)
Async XLA Ops:
  7.2 123.9 %copy-start = (bf16[4,768,256]{2,1,0:T(8,128)(2,1)S(1)}, bf16[4,768,256]{2,1,0:T(8,128)(2,1)}, u32[]{:S(2)}) copy-start(bf16[4,768,256]{2,1,0:T(8,128)(2,1)} %param.12) | copy-start | bytes 4718596
  7.2 238.6 %all-reduce.2.cloned.1.call-start = ((), (), s32[]{:S(2)}) async-start(), calls=%async_computation.5 | async-start | bytes 6291456 | tf_op jit(solution)/shard_map/psum | solution.py:51
  32.4 8.7 %copy-start.2 = (bf16[128,256]{1,0:T(8,128)(2,1)S(1)}, bf16[128,256]{1,0:T(8,128)(2,1)}, u32[]{:S(2)}) copy-start(bf16[128,256]{1,0:T(8,128)(2,1)} %param.7) | copy-start | bytes 196612
  48.6 36.2 %copy-start.7 = (bf16[4,256,768]{2,1,0:T(8,128)(2,1)S(1)}, bf16[4,256,768]{2,1,0:T(8,128)(2,1)}, u32[]{:S(2)}) copy-start(bf16[4,256,768]{2,1,0:T(8,128)(2,1)} %param.10) | copy-start | bytes 4718596
  84.8 2.7 copy-start.3
  87.5 4.2 copy-start.1
  87.5 432.2 %all-gather.4.cloned.1.call-start = ((), (), s32[]{:S(2)}) async-start(), calls=%async_computation.6 | async-start | bytes 53477376 | tf_op jit(solution)/shard_map/all_gather | solution.py:52
  91.6 512.8 %reduce-scatter.2.cloned.1.call-start = ((), (), s32[]{:S(2)}) async-start(), calls=%async_computation.7 | async-start | bytes 3342336 | tf_op jit(solution)/shard_map/reduce_scatter | solution.py:66
  133.8 530.0 %all-gather.6.cloned.1.call-start = ((), (), s32[]{:S(2)}) async-start(), calls=%async_computation.8 | async-start | bytes 3342336 | tf_op jit(solution)/shard_map/all_gather | solution.py:75
  606.6 116.6 %all-gather.8.cloned.1.call-start = ((), (), s32[]{:S(2)}) async-start(), calls=%async_computation.9 | async-start | bytes 3342336 | tf_op jit(solution)/shard_map/all_gather | solution.py:76
  611.0 1.7 copy-start.6
  613.7 114.5 %all-to-all-start.1 = ((bf16[4,16,32,256]{3,2,0,1:T(8,128)(2,1)}), bf16[4,16,32,256]{3,2,0,1:T(8,128)(2,1)}, u32[]{:S(2)}, u32[]{:S(2)}) async-start(bf16[4,16,32,256]{3,2,0,1:T(8,128)(2,1)} %copy.55), calls=%async_computation.1 | async-start | bytes 2097152 | tf_op jit(solution)/shard_map/all_to_all | solution.py:149
  728.3 94.6 %all-to-all-start.3 = ((bf16[4,16,32,256]{3,2,0,1:T(8,128)(2,1)}), bf16[4,16,32,256]{3,2,0,1:T(8,128)(2,1)}, u32[]{:S(2)}, u32[]{:S(2)}) async-start(bf16[4,16,32,256]{3,2,0,1:T(8,128)(2,1)} %copy.61), calls=%async_computation.4 | async-start | bytes 2097152 | tf_op jit(solution)/shard_map/all_to_all | solution.py:150
  746.5 74.1 %copy-start.4 = (bf16[4,16,32,256]{3,2,1,0:T(8,128)(2,1)S(1)}, bf16[4,16,32,256]{3,2,1,0:T(8,128)(2,1)}, u32[]{:S(2)}) copy-start(bf16[4,16,32,256]{3,2,1,0:T(8,128)(2,1)} %copy-done.3) | copy-start | bytes 3145732
  816.1 4.5 copy-start.5
Sparse Core Ops, SparseCore 0:
  87.6 158.1 all-reduce.1
  248.5 271.1 all-gather.3
  524.0 80.3 reduce-scatter.1
  607.0 56.7 all-gather.5
  666.9 56.2 all-gather.7
